TPU v7x, 256 devices: a whole 4x4x8 slice. The times are simulated.
256 devices in a mesh: row: 32 (over z_lo, y, x), col: 8 (over z_hi, core).
Axes of the slice: x: 4, y: 4, z: 8 (z_hi: 4, z_lo: 2; z = z_hi * 2 + z_lo), core: 2. Of those that a mesh axis runs over, the one named last changes fastest.
Arguments:
- positions: float32 [3, 14336], P(None, ('row', 'col')), as said below
- polarizability: float32 [14336], P(('row', 'col')), may hold values from 0.04 to 0.16
- seeds: float32 [3, 16, 14336], P(None, None, ('row', 'col')), may hold values from -6 to 6
- dipoles: float32 [3, 16, 14336], P(None, None, ('row', 'col')), may hold values from -1.8 to 1.8
- tile_mask: int32 [256, 256], P('row', 'col'), may hold values from 0 to 1, as said below
Outputs:
- adjoint_field: float32 [3, 16, 14336], P(None, None, ('row', 'col'))
- gradient: float32 [3, 14336], P(None, ('row', 'col'))
Inputs may be any that keep to these rules, and one draw needn't show every extreme that they name: `positions`: beads lie near distinct points of a unit cubic lattice, each coordinate within 0.3 of its point; the points fill a roughly spherical droplet, and the beads of one block are spatially compact clusters of neighbouring points. Read as m_ab = tile_mask[a, (b % 8) * 32 + b // 8], m_ab is 1 exactly when the axis-aligned boxes spanned by the lattice points of blocks a and b lie within a distance of 6 of each other; so the table is symmetric with ones on the diagonal.
All inputs are finite; a program needn't handle non-finite values.
Results may differ from a plain program's by a relative error of at most 0.0003.
Values sent between devices are 32-bit elements; how exact they have to be, the bound alone decides.
No kernel may reach another device: no remote copies, remote signals or barrier semaphores. Data moves between devices by JAX's collectives and lax.ppermute only.
A program may use at most 64 MiB of HBM per device.

v0:
```python
import jax
import jax.numpy as jnp
from jax import lax
from jax.sharding import PartitionSpec as P

THOLE_DAMPING = 0.39
HIGHEST = lax.Precision.HIGHEST


def cut_along(x, dim, devices):
    before, after = (x.shape[:dim], x.shape[dim + 1 :])
    return jnp.moveaxis(x.reshape(*before, devices, -1, *after), dim, 0)


def sent_and_summed(x, axis, dim):
    pieces = cut_along(x, dim, lax.axis_size(axis))
    arrived = lax.all_to_all(pieces, axis, split_axis=0, concat_axis=0, tiled=True)
    return arrived.sum(axis=0)


def rows_first(arrays, axis, dims):
    turned = [jnp.moveaxis(a, dim, 0) for a, dim in zip(arrays, dims)]
    widths = [t[0].size for t in turned]
    both = jnp.concatenate([t.reshape(-1, w) for t, w in zip(turned, widths)], axis=1)
    out = lax.all_gather(both, axis, axis=0, tiled=True)
    pieces = jnp.split(out, [sum(widths[:k]) for k in range(1, len(widths))], axis=1)
    return tuple(
        (
            jnp.moveaxis(b.reshape(-1, *t.shape[1:]), 0, dim)
            for b, t, dim in zip(pieces, turned, dims)
        )
    )


def from_everyone(x, axis):
    devices = lax.axis_size(axis)
    return lax.all_to_all(jnp.broadcast_to(x[None], (devices, *x.shape)), axis, 0, 0, tiled=True)


def laid_out(pieces, dim):
    dims = list(pieces.shape[1:])
    dims[dim] *= pieces.shape[0]
    return jnp.moveaxis(pieces, 0, dim).reshape(dims)


def gathered_copies(x, axis, dim):
    pieces = from_everyone(x, axis)
    return laid_out(pieces, dim)


def pair_terms(row_geom, col_geom, keep_mask):
    offset = row_geom[:3, :, None] - col_geom[:3, None, :]
    dist_sq = jnp.sum(offset * offset, axis=0)
    dist_sq = jnp.where(keep_mask > 0.0, dist_sq, 1.0)
    inverse = lax.rsqrt(dist_sq)
    damping = (
        THOLE_DAMPING * dist_sq * (dist_sq * inverse) * row_geom[3][:, None] * col_geom[3][None, :]
    )
    damp_exp = jnp.exp(-damping)
    inv_cube = keep_mask * inverse * inverse * inverse
    isotropic = (1.0 - damp_exp) * inv_cube
    radial = 3.0 * (1.0 - (1.0 + damping) * damp_exp) * inv_cube * inverse * inverse
    tensor = radial[None, None] * offset[:, None] * offset[None, :]
    return (tensor, isotropic)


def apply_rows(tensor, isotropic, vector):
    result = jnp.einsum("abij,bpj->api", tensor, vector, precision=HIGHEST)
    return result - jnp.einsum("ij,apj->api", isotropic, vector, precision=HIGHEST)


def apply_cols(tensor, isotropic, vector):
    result = jnp.einsum("abij,bpi->apj", tensor, vector, precision=HIGHEST)
    return result - jnp.einsum("ij,api->apj", isotropic, vector, precision=HIGHEST)


def split_rows(values, groups):
    shaped = values.reshape(values.shape[:-1] + (groups, values.shape[-1] // groups))
    return jnp.moveaxis(shaped, -2, 0)


def join_rows(values):
    shifted = jnp.moveaxis(values, 0, -2)
    return shifted.reshape(shifted.shape[:-2] + (-1,))


def local(positions, polarizability, seeds, dipoles, tile_mask):
    bead_count = positions.shape[1]
    probes = seeds.shape[1]
    row_count = lax.axis_size("row")
    col_count = lax.axis_size("col")
    row_at = lax.axis_index("row")
    col_at = lax.axis_index("col")
    span_cols = bead_count * row_count
    geometry = jnp.concatenate([positions, lax.rsqrt(polarizability)[None, :]], axis=0)
    start_vector = polarizability[None, None, :] * seeds
    col_slot = jnp.arange(span_cols, dtype=jnp.int32)
    col_group = col_slot // bead_count
    col_global = (col_group * col_count + col_at) * bead_count + col_slot % bead_count
    row_global = (row_at * col_count + jnp.arange(col_count, dtype=jnp.int32))[:, None] * bead_count
    row_global = row_global + jnp.arange(bead_count, dtype=jnp.int32)[None, :]
    selector = (col_group[None, :] == jnp.arange(row_count, dtype=jnp.int32)[:, None]).astype(
        jnp.float32
    )
    col_mask = jnp.dot(tile_mask.astype(jnp.float32), selector, precision=HIGHEST)
    keep_mask = col_mask[:, None, :] * (row_global[:, :, None] != col_global[None, None, :]).astype(
        jnp.float32
    )

    def sweep_cols(vector_rows_split, rows_split, geom_cols):

        def one_shard(running, inputs):
            geom_rows, keep_rows, vector_rows = inputs
            tensor, isotropic = pair_terms(geom_rows, geom_cols, keep_rows)
            return (running + apply_cols(tensor, isotropic, vector_rows), None)

        empty_sum = jnp.zeros((3, probes, span_cols), jnp.float32)
        partial_cols, ignored = lax.scan(
            one_shard, empty_sum, (rows_split, keep_mask, vector_rows_split)
        )
        return sent_and_summed(partial_cols, "row", 2)

    geom_rows_all, start_rows = rows_first((geometry, start_vector), "col", (1, 2))
    geom_cols, dipole_cols = rows_first((geometry, dipoles), "row", (1, 2))
    rows_split = split_rows(geom_rows_all, col_count)
    field_one = seeds + sweep_cols(split_rows(start_rows, col_count), rows_split, geom_cols)
    next_vector = polarizability[None, None, :] * field_one
    next_rows = gathered_copies(next_vector, "col", 2)
    field_two = seeds + sweep_cols(split_rows(next_rows, col_count), rows_split, geom_cols)
    adjoint = polarizability[None, None, :] * field_two
    adjoint_rows = gathered_copies(adjoint, "col", 2)

    def pair_score(geom_rows, geom_all, keep_rows, adjoint_one):
        tensor, isotropic = pair_terms(geom_rows, geom_all, keep_rows)
        return jnp.sum(adjoint_one * apply_rows(tensor, isotropic, dipole_cols))

    slopes = jax.grad(pair_score, argnums=(0, 1))

    def force_shard(running, inputs):
        geom_rows, keep_rows, adjoint_one = inputs
        slope_rows, slope_cols = slopes(geom_rows, geom_cols, keep_rows, adjoint_one)
        return (running + slope_cols[:3], slope_rows[:3])

    empty_force = jnp.zeros((3, span_cols), jnp.float32)
    force_cols, force_split = lax.scan(
        force_shard, empty_force, (rows_split, keep_mask, split_rows(adjoint_rows, col_count))
    )
    force_rows = join_rows(force_split)
    gradient = sent_and_summed(force_rows, "col", 1) + sent_and_summed(force_cols, "row", 1)
    return (field_two, gradient)


def solution(mesh):
    in_specs = (
        P(None, ("row", "col")),
        P(("row", "col")),
        P(None, None, ("row", "col")),
        P(None, None, ("row", "col")),
        P("row", "col"),
    )
    out_specs = (P(None, None, ("row", "col")), P(None, ("row", "col")))
    return jax.shard_map(local, mesh=mesh, in_specs=in_specs, out_specs=out_specs, check_vma=False)
```

profile of v0, /device:TPU:1, one launch (start us, length us, event | category | flops | bytes accessed | tf_op | source)
XLA Modules:
  0.0 371.4 jit_solution(5194163001965535177)
XLA Ops:
  3.7 73.9 %all_gather.7 = f32[1792,52]{1,0:T(8,128)S(1)} all-gather(f32[56,52]{1,0:T(8,128)S(1)} %copy.28), channel_id=1, replica_groups=mesh['row'=32,'col'=8] {'row'}, dimensions={0}, use_global_device_ids=true | all-gather | bytes 384384 | tf_op jit(solution)/shard_map/all_gather | solution.py:25
  78.1 31.7 %all_gather.6 = f32[448,52]{1,0:T(8,128)S(1)} all-gather(f32[56,52]{1,0:T(8,128)S(1)} %copy.25), channel_id=1, replica_groups=mesh['row'=32,'col'=8] {'col'}, dimensions={0}, use_global_device_ids=true | all-gather | bytes 104832 | tf_op jit(solution)/shard_map/all_gather | solution.py:25
  112.4 44.9 %while.35 = (s32[]{:T(128)}, f32[3,16,1792]{2,1,0:T(8,128)S(1)}, f32[8,3,16,56]{3,0,2,1:T(8,128)S(1)}, f32[8,56,1792]{2,1,0:T(8,128)}, f32[8,4,56]{2,1,0:T(4,128...) while((s32[]{:T(128)}, f32[3,16,1792]{2,1,0:T(8,128)S(1)}, ...), condition=%wide.region_2.3_spmd.clone, body=%wide.region_0.2_spmd.clone.sunk | while | flops 236888064 | bytes 9123691 | solution.py:118
  114.2 2.1 fusion.132
  119.9 2.1 fusion.132
  125.5 2.1 fusion.132
  131.1 2.1 fusion.132
  136.7 2.1 fusion.132
  142.3 2.1 fusion.132
  147.9 2.1 fusion.132
  153.6 2.1 fusion.132
  159.5 12.1 %all_to_all.30 = f32[32,1,2688]{2,1,0:T(1,128)S(1)} all-to-all(f32[32,1,2688]{2,1,0:T(1,128)S(1)} %reshape.386), channel_id=1, replica_groups=mesh['row'=32,'col'=8] {'row'}, dimensions={0} | all-to-all | bytes 688128 | tf_op jit(solution)/shard_map/all_to_all | solution.py:17
  175.1 6.4 %all-to-all-start.1 = ((f32[8,1,2688]{2,1,0:T(1,128)}), f32[8,1,2688]{2,1,0:T(1,128)S(1)}, u32[]{:S(2)}, u32[]{:S(2)}) async-start(f32[8,1,2688]{2,1,0:T(1,128)} %reshape.388), calls=%async_computation.1 | async-start | bytes 172032 | tf_op jit(solution)/shard_map/all_to_all | solution.py:37
  181.6 7.6 %all-to-all-done.1 = f32[8,1,2688]{2,1,0:T(1,128)S(1)} async-done(((f32[8,1,2688]{2,1,0:T(1,128)}), f32[8,1,2688]{2,1,0:T(1,128)S(1)}, u32[]{:S(2)}, u32[]{:S(2)}) %all-to-all-start.1) | async-done | bytes 86048 | tf_op jit(solution)/shard_map/all_to_all | solution.py:37
  190.1 44.6 %while.36 = (s32[]{:T(128)}, f32[3,16,1792]{2,1,0:T(8,128)S(1)}, f32[8,3,16,56]{3,2,1,0:T(8,128)S(1)}, f32[8,56,1792]{2,1,0:T(8,128)}, f32[8,4,56]{2,1,0:T(4,128...) while((s32[]{:T(128)}, f32[3,16,1792]{2,1,0:T(8,128)S(1)}, ...), condition=%wide.region_6.7_spmd.clone, body=%wide.region_4.6_spmd.clone.sunk | while | flops 236888064 | bytes 9131659 | solution.py:118
  197.5 2.0 fusion.138
  236.8 12.2 %all_to_all.31 = f32[32,1,2688]{2,1,0:T(1,128)S(1)} all-to-all(f32[32,1,2688]{2,1,0:T(1,128)S(1)} %reshape.390), channel_id=1, replica_groups=mesh['row'=32,'col'=8] {'row'}, dimensions={0} | all-to-all | bytes 688128 | tf_op jit(solution)/shard_map/all_to_all | solution.py:17
  252.6 5.5 %all-to-all-start.3 = ((f32[8,1,2688]{2,1,0:T(1,128)}), f32[8,1,2688]{2,1,0:T(1,128)S(1)}, u32[]{:S(2)}, u32[]{:S(2)}) async-start(f32[8,1,2688]{2,1,0:T(1,128)} %reshape.392), calls=%async_computation.3 | async-start | bytes 172032 | tf_op jit(solution)/shard_map/all_to_all | solution.py:37
  258.7 7.0 %all-to-all-done.3 = f32[8,1,2688]{2,1,0:T(1,128)S(1)} async-done(((f32[8,1,2688]{2,1,0:T(1,128)}), f32[8,1,2688]{2,1,0:T(1,128)S(1)}, u32[]{:S(2)}, u32[]{:S(2)}) %all-to-all-start.3) | async-done | bytes 86048 | tf_op jit(solution)/shard_map/all_to_all | solution.py:37
  266.8 80.1 %while.37 = (s32[]{:T(128)}, f32[3,1792]{1,0:T(4,128)S(1)}, f32[8,3,56]{2,1,0:T(4,128)S(1)}, f32[8,56,1792]{2,1,0:T(8,128)}, f32[8,4,56]{2,1,0:T(4,128)S(1)}, /*...) while((s32[]{:T(128)}, f32[3,1792]{1,0:T(4,128)S(1)}, ...), condition=%wide.region_17.18_spmd.clone, body=%wide.region_8.17_spmd.clone.sunk | while | flops 248187520 | bytes 19899200 | solution.py:145
  268.6 3.7 fusion.142
  278.6 3.7 fusion.142
  288.6 3.7 fusion.142
  298.6 3.7 fusion.142
  308.6 3.7 fusion.142
  318.6 3.7 fusion.142
  328.6 3.7 fusion.142
  338.6 3.7 fusion.142
  347.5 4.3 %all-to-all-start.4 = ((f32[8,1,168]{2,1,0:T(1,128)}), f32[8,1,168]{2,1,0:T(1,128)S(1)}, u32[]{:S(2)}, u32[]{:S(2)}) async-start(f32[8,1,168]{2,1,0:T(1,128)} %reshape.394), calls=%async_computation.4 | async-start | bytes 16384 | tf_op jit(solution)/shard_map/all_to_all | solution.py:17
  352.7 6.2 %all-to-all-done.4 = f32[8,1,168]{2,1,0:T(1,128)S(1)} async-done(((f32[8,1,168]{2,1,0:T(1,128)}), f32[8,1,168]{2,1,0:T(1,128)S(1)}, u32[]{:S(2)}, u32[]{:S(2)}) %all-to-all-start.4) | async-done | bytes 5408 | tf_op jit(solution)/shard_map/all_to_all | solution.py:17
  358.9 3.9 %all-to-all-start.5 = ((f32[32,1,168]{2,1,0:T(1,128)}), f32[32,1,168]{2,1,0:T(1,128)S(1)}, u32[]{:S(2)}, u32[]{:S(2)}) async-start(f32[32,1,168]{2,1,0:T(1,128)} %reshape.396), calls=%async_computation.5 | async-start | bytes 65536 | tf_op jit(solution)/shard_map/all_to_all | solution.py:17
  363.5 6.4 %all-to-all-done.5 = f32[32,1,168]{2,1,0:T(1,128)S(1)} async-done(((f32[32,1,168]{2,1,0:T(1,128)}), f32[32,1,168]{2,1,0:T(1,128)S(1)}, u32[]{:S(2)}, u32[]{:S(2)}) %all-to-all-start.5) | async-done | bytes 21536 | tf_op jit(solution)/shard_map/all_to_all | solution.py:17
  (335 shorter events, 143.5 us)
Async XLA Ops:
  77.7 32.6 %copy-start.2 = (s32[8,32]{1,0:T(8,128)S(1)}, s32[8,32]{1,0:T(8,128)}, u32[]{:S(2)}) copy-start(s32[8,32]{1,0:T(8,128)} %param.15) | copy-start | bytes 3076
  172.1 2.1 copy-start
  172.1 2.2 copy-start.1
  175.1 14.0 %all-to-all-start.1 = ((f32[8,1,2688]{2,1,0:T(1,128)}), f32[8,1,2688]{2,1,0:T(1,128)S(1)}, u32[]{:S(2)}, u32[]{:S(2)}) async-start(f32[8,1,2688]{2,1,0:T(1,128)} %reshape.388), calls=%async_computation.1 | async-start | bytes 172032 | tf_op jit(solution)/shard_map/all_to_all | solution.py:37
  252.6 13.1 %all-to-all-start.3 = ((f32[8,1,2688]{2,1,0:T(1,128)}), f32[8,1,2688]{2,1,0:T(1,128)S(1)}, u32[]{:S(2)}, u32[]{:S(2)}) async-start(f32[8,1,2688]{2,1,0:T(1,128)} %reshape.392), calls=%async_computation.3 | async-start | bytes 172032 | tf_op jit(solution)/shard_map/all_to_all | solution.py:37
  347.5 11.3 %all-to-all-start.4 = ((f32[8,1,168]{2,1,0:T(1,128)}), f32[8,1,168]{2,1,0:T(1,128)S(1)}, u32[]{:S(2)}, u32[]{:S(2)}) async-start(f32[8,1,168]{2,1,0:T(1,128)} %reshape.394), calls=%async_computation.4 | async-start | bytes 16384 | tf_op jit(solution)/shard_map/all_to_all | solution.py:17
  358.9 11.1 %all-to-all-start.5 = ((f32[32,1,168]{2,1,0:T(1,128)}), f32[32,1,168]{2,1,0:T(1,128)S(1)}, u32[]{:S(2)}, u32[]{:S(2)}) async-start(f32[32,1,168]{2,1,0:T(1,128)} %reshape.396), calls=%async_computation.5 | async-start | bytes 65536 | tf_op jit(solution)/shard_map/all_to_all | solution.py:17
where the time goes:
time: 374 us; the launch traced here: 371 us
  blocking collectives  130 us (35%)
  matrix products  105 us (28%)
  other arithmetic  72.7 us (19%)
  waiting for transfers between devices  27.2 us (7%)
  starting transfers between devices  20.1 us (5%)
  local copies, waits for them, and re-layouts  13.2 us (4%)
    all_gather x2, blocking collectives, rows_first(): out = lax.all_gather(both, axis, axis=0, tiled=True)  106 us
    dot_general x16, matrix products, apply_cols(): result = jnp.einsum('abij,bpi->apj', tensor, vector, precision=HIGHEST)  32.8 us
    mul x24, other arithmetic, pair_terms(): 3.0 * (1.0 - (1.0 + damping) * damp_exp) * inv_cube * inverse * inverse  31 us
    dot_general x8, matrix products, apply_rows(): result = jnp.einsum('abij,bpj->api', tensor, vector, precision=HIGHEST)  29.3 us
    dot_general x16, matrix products, apply_cols(): jnp.einsum('ij,api->apj', isotropic, vector, precision=HIGHEST)  27.4 us
    all_to_all x2, blocking collectives, sent_and_summed(): lax.all_to_all(pieces, axis, split_axis=0, concat_axis=0, tiled=True)  24.3 us
    dot_general x8, matrix products, apply_rows(): jnp.einsum('ij,apj->api', isotropic, vector, precision=HIGHEST)  15.7 us
    all_to_all x2, waiting for transfers between devices, from_everyone(): lax.all_to_all(jnp.broadcast_to(x[None], (devices, *x.shape)), axis, 0, 0...  14.6 us
  transfers between devices with their start and end apart: 4, of which 4 were waited for; matrix products, arithmetic and copies ran while one was open for 1% of the time, Pallas kernels for 0%

commit v1 on v0

--- a/solution.py
+++ b/solution.py
@@ -22,7 +22,9 @@
     turned = [jnp.moveaxis(a, dim, 0) for a, dim in zip(arrays, dims)]
     widths = [t[0].size for t in turned]
     both = jnp.concatenate([t.reshape(-1, w) for t, w in zip(turned, widths)], axis=1)
-    out = lax.all_gather(both, axis, axis=0, tiled=True)
+    out = jnp.concatenate(
+        lax.all_to_all(jnp.stack([both] * lax.axis_size(axis)), axis, 0, 0), axis=0
+    )
     pieces = jnp.split(out, [sum(widths[:k]) for k in range(1, len(widths))], axis=1)
     return tuple(
         (

time: 374 us -> 304 us (0.81)
  blocking collectives: 130 us -> 24.4 us
  starting transfers between devices: 20.1 us -> 38 us
  waiting for transfers between devices: 27.2 us -> 37.8 us
    all_gather x2 -> x0, blocking collectives: 106 us -> none  [rows_first(): out = lax.all_gather(both, axis, axis=0, tiled=True)]
    all_to_all x0 -> x2, starting transfers between devices: none -> 17.4 us  [rows_first(): lax.all_to_all(jnp.stack([both] * lax.axis_size(axis)), axis, 0, 0)]
    all_to_all x0 -> x2, waiting for transfers between devices: none -> 10 us  [rows_first(): lax.all_to_all(jnp.stack([both] * lax.axis_size(axis)), axis, 0, 0)]
    unnamed x22 -> x25, local copies, waits for them, and re-layouts: 7.47 us -> 9.89 us
  transfers between devices with their start and end apart: 4 -> 6, of which waited for: 4 -> 6; matrix products, arithmetic and copies ran while one was open for 1% -> 3% of each run, Pallas kernels for 0% -> 0%
where the time goes in v1:
time: 304 us; the launch traced here: 300 us
  matrix products  106 us (35%)
  other arithmetic  75.2 us (25%)
  starting transfers between devices  38 us (12%)
  waiting for transfers between devices  37.8 us (12%)
  blocking collectives  24.4 us (8%)
  local copies, waits for them, and re-layouts  15.9 us (5%)
    dot_general x16, matrix products, apply_cols(): result = jnp.einsum('abij,bpi->apj', tensor, vector, precision=HIGHEST)  33 us
    mul x24, other arithmetic, pair_terms(): 3.0 * (1.0 - (1.0 + damping) * damp_exp) * inv_cube * inverse * inverse  30.9 us
    dot_general x8, matrix products, apply_rows(): result = jnp.einsum('abij,bpj->api', tensor, vector, precision=HIGHEST)  29.9 us
    dot_general x16, matrix products, apply_cols(): jnp.einsum('ij,api->apj', isotropic, vector, precision=HIGHEST)  27.5 us
    all_to_all x2, blocking collectives, sent_and_summed(): lax.all_to_all(pieces, axis, split_axis=0, concat_axis=0, tiled=True)  24.4 us
    all_to_all x2, starting transfers between devices, rows_first(): lax.all_to_all(jnp.stack([both] * lax.axis_size(axis)), axis, 0, 0)  17.4 us
    dot_general x8, matrix products, apply_rows(): jnp.einsum('ij,apj->api', isotropic, vector, precision=HIGHEST)  15.7 us
    all_to_all x2, waiting for transfers between devices, from_everyone(): lax.all_to_all(jnp.broadcast_to(x[None], (devices, *x.shape)), axis, 0, 0...  15.1 us
  transfers between devices with their start and end apart: 6, of which 6 were waited for; matrix products, arithmetic and copies ran while one was open for 3% of the time, Pallas kernels for 0%

profile of v1, /device:TPU:1, one launch (start us, length us, event | category | flops | bytes accessed | tf_op | source)
XLA Modules:
  0.0 300.5 jit_solution(1577313185306925809)
XLA Ops:
  4.4 10.0 %all-to-all-start = ((f32[8,1,2912]{2,1,0:T(1,128)}), f32[8,1,2912]{2,1,0:T(1,128)S(1)}, u32[]{:S(2)}, u32[]{:S(2)}) async-start(f32[8,1,2912]{2,1,0:T(1,128)} %reshape.398), calls=%async_computation | async-start | bytes 188416 | tf_op jit(solution)/shard_map/all_to_all | solution.py:26
  16.5 5.5 %all-to-all-done = f32[8,1,2912]{2,1,0:T(1,128)S(1)} async-done(((f32[8,1,2912]{2,1,0:T(1,128)}), f32[8,1,2912]{2,1,0:T(1,128)S(1)}, u32[]{:S(2)}, u32[]{:S(2)}) %all-to-all-start) | async-done | bytes 93216 | tf_op jit(solution)/shard_map/all_to_all | solution.py:26
  22.0 7.5 %all-to-all-start.1 = ((f32[32,1,2912]{2,1,0:T(1,128)}), f32[32,1,2912]{2,1,0:T(1,128)S(1)}, u32[]{:S(2)}, u32[]{:S(2)}) async-start(f32[32,1,2912]{2,1,0:T(1,128)} %reshape.400), calls=%async_computation.1 | async-start | bytes 753664 | tf_op jit(solution)/shard_map/all_to_all | solution.py:26
  33.4 4.5 %all-to-all-done.1 = f32[32,1,2912]{2,1,0:T(1,128)S(1)} async-done(((f32[32,1,2912]{2,1,0:T(1,128)}), f32[32,1,2912]{2,1,0:T(1,128)S(1)}, u32[]{:S(2)}, u32[]{:S(2)}) %all-to-all-start.1) | async-done | bytes 372768 | tf_op jit(solution)/shard_map/all_to_all | solution.py:26
  40.6 45.0 %while.35 = (s32[]{:T(128)}, f32[3,16,1792]{2,1,0:T(8,128)S(1)}, f32[8,3,16,56]{3,0,2,1:T(8,128)S(1)}, f32[8,56,1792]{2,1,0:T(8,128)}, f32[8,4,56]{2,1,0:T(4,128...) while((s32[]{:T(128)}, f32[3,16,1792]{2,1,0:T(8,128)S(1)}, ...), condition=%wide.region_2.3_spmd.clone, body=%wide.region_0.2_spmd.clone.sunk | while | flops 236888064 | bytes 9123691 | solution.py:120
  42.4 2.1 fusion.132
  48.0 2.1 fusion.132
  53.6 2.1 fusion.132
  59.3 2.1 fusion.132
  70.5 2.1 fusion.132
  76.1 2.1 fusion.132
  81.7 2.1 fusion.132
  87.7 12.1 %all_to_all.40 = f32[32,1,2688]{2,1,0:T(1,128)S(1)} all-to-all(f32[32,1,2688]{2,1,0:T(1,128)S(1)} %reshape.402), channel_id=1, replica_groups=mesh['row'=32,'col'=8] {'row'}, dimensions={0} | all-to-all | bytes 688128 | tf_op jit(solution)/shard_map/all_to_all | solution.py:17
  102.8 6.8 %all-to-all-start.3 = ((f32[8,1,2688]{2,1,0:T(1,128)}), f32[8,1,2688]{2,1,0:T(1,128)S(1)}, u32[]{:S(2)}, u32[]{:S(2)}) async-start(f32[8,1,2688]{2,1,0:T(1,128)} %reshape.404), calls=%async_computation.3 | async-start | bytes 172032 | tf_op jit(solution)/shard_map/all_to_all | solution.py:39
  109.7 7.6 %all-to-all-done.3 = f32[8,1,2688]{2,1,0:T(1,128)S(1)} async-done(((f32[8,1,2688]{2,1,0:T(1,128)}), f32[8,1,2688]{2,1,0:T(1,128)S(1)}, u32[]{:S(2)}, u32[]{:S(2)}) %all-to-all-start.3) | async-done | bytes 86048 | tf_op jit(solution)/shard_map/all_to_all | solution.py:39
  118.2 44.6 %while.36 = (s32[]{:T(128)}, f32[3,16,1792]{2,1,0:T(8,128)S(1)}, f32[8,3,16,56]{3,2,1,0:T(8,128)S(1)}, f32[8,56,1792]{2,1,0:T(8,128)}, f32[8,4,56]{2,1,0:T(4,128...) while((s32[]{:T(128)}, f32[3,16,1792]{2,1,0:T(8,128)S(1)}, ...), condition=%wide.region_6.7_spmd.clone, body=%wide.region_4.6_spmd.clone.sunk | while | flops 236888064 | bytes 9131659 | solution.py:120
  165.0 12.3 %all_to_all.41 = f32[32,1,2688]{2,1,0:T(1,128)S(1)} all-to-all(f32[32,1,2688]{2,1,0:T(1,128)S(1)} %reshape.406), channel_id=1, replica_groups=mesh['row'=32,'col'=8] {'row'}, dimensions={0} | all-to-all | bytes 688128 | tf_op jit(solution)/shard_map/all_to_all | solution.py:17
  180.9 5.5 %all-to-all-start.5 = ((f32[8,1,2688]{2,1,0:T(1,128)}), f32[8,1,2688]{2,1,0:T(1,128)S(1)}, u32[]{:S(2)}, u32[]{:S(2)}) async-start(f32[8,1,2688]{2,1,0:T(1,128)} %reshape.408), calls=%async_computation.5 | async-start | bytes 172032 | tf_op jit(solution)/shard_map/all_to_all | solution.py:39
  186.4 7.5 %all-to-all-done.5 = f32[8,1,2688]{2,1,0:T(1,128)S(1)} async-done(((f32[8,1,2688]{2,1,0:T(1,128)}), f32[8,1,2688]{2,1,0:T(1,128)S(1)}, u32[]{:S(2)}, u32[]{:S(2)}) %all-to-all-start.5) | async-done | bytes 86048 | tf_op jit(solution)/shard_map/all_to_all | solution.py:39
  195.0 81.0 %while.37 = (s32[]{:T(128)}, f32[3,1792]{1,0:T(4,128)S(1)}, f32[8,3,56]{2,1,0:T(4,128)S(1)}, f32[8,56,1792]{2,1,0:T(8,128)}, f32[8,4,56]{2,1,0:T(4,128)S(1)}, /*...) while((s32[]{:T(128)}, f32[3,1792]{1,0:T(4,128)S(1)}, ...), condition=%wide.region_17.18_spmd.clone, body=%wide.region_8.17_spmd.clone.sunk | while | flops 248187520 | bytes 19899200 | solution.py:147
  196.8 3.7 %fusion.142 = (f32[3,56,1792]{2,1,0:T(8,128)S(1)}, f32[3,56,1792]{2,1,0:T(8,128)S(1)}) fusion(f32[3,56,1792]{2,1,0:T(8,128)S(1)} %get-tuple-element.447, f32[3,56,1792]{2,1,0:T(8,128)S(1)} %get-tuple-element.448, f32[3,16,1792]{2,1,0:T(8,128)S(1)} %get-tuple-element.532, f32[8,3,16,56]{3,2,1,0:T(8,128)S(1)} %get-tuple-element.531, ...), kind=kOutput, calls=%fused_computation.99.clone.1 | convolution fusion | flops 176418816 | bytes 5185540 | tf_op jit(solution)/shard_map/while/body/eval_jaxpr/transpose(jvp(abij,bpj->api))/dot_general | solution.py:70
  206.9 3.7 %fusion.142 = (f32[3,56,1792]{2,1,0:T(8,128)S(1)}, f32[3,56,1792]{2,1,0:T(8,128)S(1)}) fusion(f32[3,56,1792]{2,1,0:T(8,128)S(1)} %get-tuple-element.447, f32[3,56,1792]{2,1,0:T(8,128)S(1)} %get-tuple-element.448, f32[3,16,1792]{2,1,0:T(8,128)S(1)} %get-tuple-element.532, f32[8,3,16,56]{3,2,1,0:T(8,128)S(1)} %get-tuple-element.531, ...), kind=kOutput, calls=%fused_computation.99.clone.1 | convolution fusion | flops 176418816 | bytes 5185540 | tf_op jit(solution)/shard_map/while/body/eval_jaxpr/transpose(jvp(abij,bpj->api))/dot_general | solution.py:70
  217.0 3.7 %fusion.142 = (f32[3,56,1792]{2,1,0:T(8,128)S(1)}, f32[3,56,1792]{2,1,0:T(8,128)S(1)}) fusion(f32[3,56,1792]{2,1,0:T(8,128)S(1)} %get-tuple-element.447, f32[3,56,1792]{2,1,0:T(8,128)S(1)} %get-tuple-element.448, f32[3,16,1792]{2,1,0:T(8,128)S(1)} %get-tuple-element.532, f32[8,3,16,56]{3,2,1,0:T(8,128)S(1)} %get-tuple-element.531, ...), kind=kOutput, calls=%fused_computation.99.clone.1 | convolution fusion | flops 176418816 | bytes 5185540 | tf_op jit(solution)/shard_map/while/body/eval_jaxpr/transpose(jvp(abij,bpj->api))/dot_general | solution.py:70
  227.1 3.7 %fusion.142 = (f32[3,56,1792]{2,1,0:T(8,128)S(1)}, f32[3,56,1792]{2,1,0:T(8,128)S(1)}) fusion(f32[3,56,1792]{2,1,0:T(8,128)S(1)} %get-tuple-element.447, f32[3,56,1792]{2,1,0:T(8,128)S(1)} %get-tuple-element.448, f32[3,16,1792]{2,1,0:T(8,128)S(1)} %get-tuple-element.532, f32[8,3,16,56]{3,2,1,0:T(8,128)S(1)} %get-tuple-element.531, ...), kind=kOutput, calls=%fused_computation.99.clone.1 | convolution fusion | flops 176418816 | bytes 5185540 | tf_op jit(solution)/shard_map/while/body/eval_jaxpr/transpose(jvp(abij,bpj->api))/dot_general | solution.py:70
  237.2 3.7 %fusion.142 = (f32[3,56,1792]{2,1,0:T(8,128)S(1)}, f32[3,56,1792]{2,1,0:T(8,128)S(1)}) fusion(f32[3,56,1792]{2,1,0:T(8,128)S(1)} %get-tuple-element.447, f32[3,56,1792]{2,1,0:T(8,128)S(1)} %get-tuple-element.448, f32[3,16,1792]{2,1,0:T(8,128)S(1)} %get-tuple-element.532, f32[8,3,16,56]{3,2,1,0:T(8,128)S(1)} %get-tuple-element.531, ...), kind=kOutput, calls=%fused_computation.99.clone.1 | convolution fusion | flops 176418816 | bytes 5185540 | tf_op jit(solution)/shard_map/while/body/eval_jaxpr/transpose(jvp(abij,bpj->api))/dot_general | solution.py:70
  247.3 3.7 %fusion.142 = (f32[3,56,1792]{2,1,0:T(8,128)S(1)}, f32[3,56,1792]{2,1,0:T(8,128)S(1)}) fusion(f32[3,56,1792]{2,1,0:T(8,128)S(1)} %get-tuple-element.447, f32[3,56,1792]{2,1,0:T(8,128)S(1)} %get-tuple-element.448, f32[3,16,1792]{2,1,0:T(8,128)S(1)} %get-tuple-element.532, f32[8,3,16,56]{3,2,1,0:T(8,128)S(1)} %get-tuple-element.531, ...), kind=kOutput, calls=%fused_computation.99.clone.1 | convolution fusion | flops 176418816 | bytes 5185540 | tf_op jit(solution)/shard_map/while/body/eval_jaxpr/transpose(jvp(abij,bpj->api))/dot_general | solution.py:70
  257.5 3.7 %fusion.142 = (f32[3,56,1792]{2,1,0:T(8,128)S(1)}, f32[3,56,1792]{2,1,0:T(8,128)S(1)}) fusion(f32[3,56,1792]{2,1,0:T(8,128)S(1)} %get-tuple-element.447, f32[3,56,1792]{2,1,0:T(8,128)S(1)} %get-tuple-element.448, f32[3,16,1792]{2,1,0:T(8,128)S(1)} %get-tuple-element.532, f32[8,3,16,56]{3,2,1,0:T(8,128)S(1)} %get-tuple-element.531, ...), kind=kOutput, calls=%fused_computation.99.clone.1 | convolution fusion | flops 176418816 | bytes 5185540 | tf_op jit(solution)/shard_map/while/body/eval_jaxpr/transpose(jvp(abij,bpj->api))/dot_general | solution.py:70
  267.6 3.7 %fusion.142 = (f32[3,56,1792]{2,1,0:T(8,128)S(1)}, f32[3,56,1792]{2,1,0:T(8,128)S(1)}) fusion(f32[3,56,1792]{2,1,0:T(8,128)S(1)} %get-tuple-element.447, f32[3,56,1792]{2,1,0:T(8,128)S(1)} %get-tuple-element.448, f32[3,16,1792]{2,1,0:T(8,128)S(1)} %get-tuple-element.532, f32[8,3,16,56]{3,2,1,0:T(8,128)S(1)} %get-tuple-element.531, ...), kind=kOutput, calls=%fused_computation.99.clone.1 | convolution fusion | flops 176418816 | bytes 5185540 | tf_op jit(solution)/shard_map/while/body/eval_jaxpr/transpose(jvp(abij,bpj->api))/dot_general | solution.py:70
  276.6 4.3 %all-to-all-start.6 = ((f32[8,1,168]{2,1,0:T(1,128)}), f32[8,1,168]{2,1,0:T(1,128)S(1)}, u32[]{:S(2)}, u32[]{:S(2)}) async-start(f32[8,1,168]{2,1,0:T(1,128)} %reshape.410), calls=%async_computation.6 | async-start | bytes 16384 | tf_op jit(solution)/shard_map/all_to_all | solution.py:17
  281.8 6.2 %all-to-all-done.6 = f32[8,1,168]{2,1,0:T(1,128)S(1)} async-done(((f32[8,1,168]{2,1,0:T(1,128)}), f32[8,1,168]{2,1,0:T(1,128)S(1)}, u32[]{:S(2)}, u32[]{:S(2)}) %all-to-all-start.6) | async-done | bytes 5408 | tf_op jit(solution)/shard_map/all_to_all | solution.py:17
  288.0 3.9 %all-to-all-start.7 = ((f32[32,1,168]{2,1,0:T(1,128)}), f32[32,1,168]{2,1,0:T(1,128)S(1)}, u32[]{:S(2)}, u32[]{:S(2)}) async-start(f32[32,1,168]{2,1,0:T(1,128)} %reshape.412), calls=%async_computation.7 | async-start | bytes 65536 | tf_op jit(solution)/shard_map/all_to_all | solution.py:17
  292.6 6.4 %all-to-all-done.7 = f32[32,1,168]{2,1,0:T(1,128)S(1)} async-done(((f32[32,1,168]{2,1,0:T(1,128)}), f32[32,1,168]{2,1,0:T(1,128)S(1)}, u32[]{:S(2)}, u32[]{:S(2)}) %all-to-all-start.7) | async-done | bytes 21536 | tf_op jit(solution)/shard_map/all_to_all | solution.py:17
  (346 shorter events, 152.9 us)
Async XLA Ops:
  0.6 13.8 %copy-start.2 = (s32[8,32]{1,0:T(8,128)S(1)}, s32[8,32]{1,0:T(8,128)}, u32[]{:S(2)}) copy-start(s32[8,32]{1,0:T(8,128)} %param.15) | copy-start | bytes 3076
  4.4 17.6 %all-to-all-start = ((f32[8,1,2912]{2,1,0:T(1,128)}), f32[8,1,2912]{2,1,0:T(1,128)S(1)}, u32[]{:S(2)}, u32[]{:S(2)}) async-start(f32[8,1,2912]{2,1,0:T(1,128)} %reshape.398), calls=%async_computation | async-start | bytes 188416 | tf_op jit(solution)/shard_map/all_to_all | solution.py:26
  22.0 16.0 %all-to-all-start.1 = ((f32[32,1,2912]{2,1,0:T(1,128)}), f32[32,1,2912]{2,1,0:T(1,128)S(1)}, u32[]{:S(2)}, u32[]{:S(2)}) async-start(f32[32,1,2912]{2,1,0:T(1,128)} %reshape.400), calls=%async_computation.1 | async-start | bytes 753664 | tf_op jit(solution)/shard_map/all_to_all | solution.py:26
  99.8 2.1 copy-start
  99.8 2.2 copy-start.1
  102.8 14.4 %all-to-all-start.3 = ((f32[8,1,2688]{2,1,0:T(1,128)}), f32[8,1,2688]{2,1,0:T(1,128)S(1)}, u32[]{:S(2)}, u32[]{:S(2)}) async-start(f32[8,1,2688]{2,1,0:T(1,128)} %reshape.404), calls=%async_computation.3 | async-start | bytes 172032 | tf_op jit(solution)/shard_map/all_to_all | solution.py:39
  180.9 13.1 %all-to-all-start.5 = ((f32[8,1,2688]{2,1,0:T(1,128)}), f32[8,1,2688]{2,1,0:T(1,128)S(1)}, u32[]{:S(2)}, u32[]{:S(2)}) async-start(f32[8,1,2688]{2,1,0:T(1,128)} %reshape.408), calls=%async_computation.5 | async-start | bytes 172032 | tf_op jit(solution)/shard_map/all_to_all | solution.py:39
  276.6 11.4 %all-to-all-start.6 = ((f32[8,1,168]{2,1,0:T(1,128)}), f32[8,1,168]{2,1,0:T(1,128)S(1)}, u32[]{:S(2)}, u32[]{:S(2)}) async-start(f32[8,1,168]{2,1,0:T(1,128)} %reshape.410), calls=%async_computation.6 | async-start | bytes 16384 | tf_op jit(solution)/shard_map/all_to_all | solution.py:17
  288.0 11.0 %all-to-all-start.7 = ((f32[32,1,168]{2,1,0:T(1,128)}), f32[32,1,168]{2,1,0:T(1,128)S(1)}, u32[]{:S(2)}, u32[]{:S(2)}) async-start(f32[32,1,168]{2,1,0:T(1,128)} %reshape.412), calls=%async_computation.7 | async-start | bytes 65536 | tf_op jit(solution)/shard_map/all_to_all | solution.py:17
